TPU v7x, 256 devices: a whole 4x4x8 slice. The times are simulated.
256 devices in a mesh: azim: 16 (over z, y_hi), rad: 8 (over x, core), axial: 2 (over y_lo).
Axes of the slice: x: 4, y: 4 (y_hi: 2, y_lo: 2; y = y_hi * 2 + y_lo), z: 8, core: 2. Of those that a mesh axis runs over, the one named last changes fastest.
Arguments:
- residual: float32 [5, 512, 128, 256], P(None, 'azim', 'rad', 'axial'), may hold values from -12 to 12
- left_vec: float32 [5, 5], replicated, may hold values from -2.5 to 2.5
- dissip: float32 [5], replicated, may hold values from 0.2 to 0.5
- azim_coef: float32 [4, 5, 512], replicated, may hold values from 0 to 1, as said below
- radial_coef: float32 [2, 5, 128], replicated, may hold values from 0 to 3328
Outputs:
- update: float32 [5, 512, 128, 256], P(None, 'azim', 'rad', 'axial')
Inputs may be any that keep to these rules, and one draw needn't show every extreme that they name: `azim_coef`: at every position a and b are positive with a + b < 1, and so are c and e with c + e < 1.
All inputs are finite; a program needn't handle non-finite values.
Results may differ from a plain program's by a relative error of at most 0.0003.
Values sent between devices are 32-bit elements; how exact they have to be, the bound alone decides.
A program may use at most 64 MiB of HBM per device.

v0:
```python
import jax
import jax.numpy as jnp
from jax import lax
from jax.sharding import PartitionSpec as P

exact_mode = lax.Precision.HIGHEST


def carried_in(part, axis, combine, identity, reverse):
    count = lax.axis_size(axis)
    place = lax.axis_index(axis)
    ahead = count - 1 - place if reverse else place
    gathered = jax.tree.map(lambda a: lax.all_gather(a, axis), part)
    state = jax.tree.map(lambda a, e: jnp.zeros_like(a) + jnp.asarray(e, a.dtype), part, identity)

    def one(hop, state):
        source = count - 1 - hop if reverse else hop
        return combine(
            state, jax.tree.map(lambda a: lax.dynamic_index_in_dim(a, source, 0, False), gathered)
        )

    return lax.fori_loop(0, ahead, one, state)


def from_root(value, axis, source):
    kept = jnp.where(lax.axis_index(axis) == source, value, 0).astype(value.dtype)
    return lax.psum(kept, axis)


def with_halo(cells, sides, width):
    for axis, dim in sides:
        count = lax.axis_size(axis)
        ends = count - 1
        head = lax.slice_in_dim(cells, 0, width, axis=dim)
        tail = lax.slice_in_dim(cells, cells.shape[dim] - width, cells.shape[dim], axis=dim)
        cells = jnp.concatenate(
            [
                lax.ppermute(tail, axis, [(i, (i + 1) % count) for i in range(ends)]),
                cells,
                lax.ppermute(head, axis, [((i + 1) % count, i) for i in range(ends)]),
            ],
            axis=dim,
        )
    return cells


def apply_map(linear_map, states):
    return jnp.einsum("fkm,fmrx->fkrx", linear_map, states, precision=exact_mode)


def compose(earlier, later):
    earlier_map, earlier_state = earlier
    later_map, later_state = later
    joined_map = jnp.einsum("fkm,fmn->fkn", later_map, earlier_map, precision=exact_mode)
    return (joined_map, apply_map(later_map, earlier_state) + later_state)


def suffix_step(running, element):
    joined = jnp.einsum("fkm,fmn->fkn", running, element, precision=exact_mode)
    return (joined, running)


def lower_inverse(first_blocks, second_blocks):
    group_len = first_blocks.shape[-1]
    identity = jnp.eye(group_len, dtype=jnp.float32)
    start = jnp.zeros(first_blocks.shape, jnp.float32)

    def row_step(carry, inputs):
        prev_one, prev_two = carry
        first_now, second_now, unit_row = inputs
        row = unit_row + first_now[..., None] * prev_one + second_now[..., None] * prev_two
        return ((row, prev_one), row)

    inputs = (jnp.moveaxis(first_blocks, -1, 0), jnp.moveaxis(second_blocks, -1, 0), identity)
    _, rows = lax.scan(row_step, (start, start), inputs)
    return jnp.moveaxis(rows, 0, -2)


def group_tables(first_coef, second_coef, ndevices, group_len):
    fields = first_coef.shape[0]
    first_blocks = jnp.transpose(first_coef.reshape(fields, ndevices, group_len), (1, 0, 2))
    second_blocks = jnp.transpose(second_coef.reshape(fields, ndevices, group_len), (1, 0, 2))
    inverses = lower_inverse(first_blocks, second_blocks)
    entry_col = (
        inverses[..., :, 0] * first_blocks[..., 0:1] + inverses[..., :, 1] * second_blocks[..., 1:2]
    )
    second_col = inverses[..., :, 0] * second_blocks[..., 0:1]
    coupling = jnp.stack([entry_col, second_col], axis=-1)
    group_maps = jnp.stack(
        [coupling[..., group_len - 1, :], coupling[..., group_len - 2, :]], axis=-2
    )
    return (inverses, coupling, group_maps)


def sweep(source, first_coef, second_coef, reverse):
    fields, group_len = (source.shape[0], source.shape[1])
    ndevices = lax.axis_size("azim")
    if reverse:
        source = jnp.flip(source, 1)
        first_coef = jnp.flip(first_coef, 1)
        second_coef = jnp.flip(second_coef, 1)
        own_index = ndevices - 1 - lax.axis_index("azim")
    else:
        own_index = lax.axis_index("azim")
    weights = jnp.sqrt(1.0 - (first_coef + second_coef) ** 2)
    own_weights = lax.dynamic_index_in_dim(
        weights.reshape(fields, ndevices, group_len), own_index, 1, keepdims=False
    )
    inverses, coupling, group_maps = group_tables(first_coef, second_coef, ndevices, group_len)
    own_inverse = lax.dynamic_index_in_dim(inverses, own_index, 0, keepdims=False)
    own_coupling = lax.dynamic_index_in_dim(coupling, own_index, 0, keepdims=False)
    own_map = lax.dynamic_index_in_dim(group_maps, own_index, 0, keepdims=False)
    local_part = jnp.einsum(
        "fij,fjrx->firx", own_inverse, source * own_weights[:, :, None, None], precision=exact_mode
    )
    own_state = jnp.stack([local_part[:, group_len - 1], local_part[:, group_len - 2]], axis=1)
    identity_map = jnp.broadcast_to(jnp.eye(2, dtype=jnp.float32), own_map.shape)
    enter_map, enter_state = carried_in(
        (own_map, own_state), "azim", compose, (identity_map, jnp.zeros_like(own_state)), reverse
    )
    closing = apply_map(own_map, enter_state) + own_state
    total_map, suffixes = lax.scan(suffix_step, identity_map, group_maps, reverse=True)
    last_device = 0 if reverse else ndevices - 1
    total_state = from_root(closing, "azim", last_device)
    loop_matrix = jnp.eye(2, dtype=jnp.float32)[None] - total_map
    determinant = (
        loop_matrix[:, 0, 0] * loop_matrix[:, 1, 1] - loop_matrix[:, 0, 1] * loop_matrix[:, 1, 0]
    )
    adjugate = jnp.stack(
        [
            jnp.stack([loop_matrix[:, 1, 1], -loop_matrix[:, 0, 1]], -1),
            jnp.stack([-loop_matrix[:, 1, 0], loop_matrix[:, 0, 0]], -1),
        ],
        -2,
    )
    start_state = apply_map(adjugate / determinant[:, None, None], total_state)
    entering = apply_map(enter_map, start_state) + enter_state
    result = local_part + jnp.einsum("fim,fmrx->firx", own_coupling, entering, precision=exact_mode)
    if reverse:
        result = jnp.flip(result, 1)
    return result


def band_inverse(below, middle, above):
    order = middle.shape[-1]
    unit = jnp.broadcast_to(jnp.eye(order, dtype=jnp.float32), middle.shape + (order,))
    return lax.linalg.tridiagonal_solve(below, middle, above, unit)


def local(residual, left_vec, dissip, azim_coef, radial_coef):
    characteristic = jnp.einsum("gf,farx->garx", left_vec, residual, precision=exact_mode)
    padded = with_halo(characteristic, (("axial", 3),), 1)
    source = characteristic + dissip[:, None, None, None] * (
        padded[..., 2:] + padded[..., :-2] - 2.0 * characteristic
    )
    lower_out = sweep(source, azim_coef[0], azim_coef[1], False)
    upper_out = sweep(lower_out, azim_coef[2], azim_coef[3], True)
    lower_rad = radial_coef[0]
    upper_rad = radial_coef[1]
    diagonal = 1.0 + lower_rad + upper_rad
    row_scale = diagonal**0.25
    below_diag = jnp.concatenate([jnp.zeros_like(lower_rad[:, :1]), -lower_rad[:, 1:]], axis=1)
    above_diag = jnp.concatenate([-upper_rad[:, :-1], jnp.zeros_like(upper_rad[:, :1])], axis=1)
    line_inverse = band_inverse(below_diag, diagonal, above_diag) * row_scale[:, None, :]
    return lax.all_to_all(
        jnp.einsum(
            "fij,fajx->faix",
            line_inverse,
            lax.all_to_all(upper_out, "rad", split_axis=1, concat_axis=2, tiled=True),
            precision=exact_mode,
        ),
        "rad",
        split_axis=2,
        concat_axis=1,
        tiled=True,
    )


def solution(mesh):
    placed = (P(None, "azim", "rad", "axial"), P(), P(), P(), P())
    return jax.shard_map(
        local,
        mesh=mesh,
        in_specs=placed,
        out_specs=P(None, "azim", "rad", "axial"),
        check_vma=False,
    )
```

profile of v0, /device:TPU:1, one launch (start us, length us, event | category | flops | bytes accessed | tf_op | source)
XLA Modules:
  0.0 1350.5 jit_solution(13215148012961599752)
XLA Ops:
  7.9 3.3 fusion.359
  11.1 2.7 fusion.554
  13.8 2.9 copy.769
  16.6 4.7 collective-permute-start.1
  21.4 2.9 copy.767
  24.2 1.7 collective-permute-start
  33.8 119.6 %while.123 = (s32[]{:T(128)}, f32[16,5,32]{2,1,0:T(8,128)}, f32[16,5,32]{2,1,0:T(8,128)S(1)}, f32[32,16,5,32]{3,2,1,0:T(8,128)}, f32[32,32]{1,0:T(8,128)}, /*ind...) while((s32[]{:T(128)}, f32[16,5,32]{2,1,0:T(8,128)}, ...), condition=%wide.region_3.4_spmd.clone, body=%wide.region_2.3_spmd.clone.sunk | while | flops 12803 | bytes 228667 | solution.py:75
  43.3 1.6 bitcast_dynamic-update-slice_fusion.11
  47.0 1.6 bitcast_dynamic-update-slice_fusion.11
  50.7 1.6 bitcast_dynamic-update-slice_fusion.11
  54.5 1.6 bitcast_dynamic-update-slice_fusion.11
  58.2 1.6 bitcast_dynamic-update-slice_fusion.11
  62.0 1.6 bitcast_dynamic-update-slice_fusion.11
  65.7 1.6 bitcast_dynamic-update-slice_fusion.11
  80.7 1.6 bitcast_dynamic-update-slice_fusion.11
  84.4 1.6 bitcast_dynamic-update-slice_fusion.11
  88.2 1.6 bitcast_dynamic-update-slice_fusion.11
  91.9 1.6 bitcast_dynamic-update-slice_fusion.11
  95.7 1.6 bitcast_dynamic-update-slice_fusion.11
  103.2 1.6 bitcast_dynamic-update-slice_fusion.11
  106.9 1.6 bitcast_dynamic-update-slice_fusion.11
  114.4 1.6 bitcast_dynamic-update-slice_fusion.11
  118.1 1.6 bitcast_dynamic-update-slice_fusion.11
  121.9 1.6 bitcast_dynamic-update-slice_fusion.11
  125.6 1.6 bitcast_dynamic-update-slice_fusion.11
  129.4 1.6 bitcast_dynamic-update-slice_fusion.11
  133.1 1.6 bitcast_dynamic-update-slice_fusion.11
  136.9 1.6 bitcast_dynamic-update-slice_fusion.11
  140.6 1.6 bitcast_dynamic-update-slice_fusion.11
  144.4 1.6 bitcast_dynamic-update-slice_fusion.11
  151.9 1.6 bitcast_dynamic-update-slice_fusion.11
  153.5 2.9 copy.773
  180.4 1.7 slice_bitcast_fusion.62
  185.9 173.1 %while.122 = (s32[]{:T(128)}, f32[16,5,32]{2,1,0:T(8,128)S(1)}, f32[16,5,32]{2,1,0:T(8,128)S(1)}, f32[32,16,5,32]{3,2,1,0:T(8,128)}, f32[32,32]{1,0:T(8,128)}, /...) while((s32[]{:T(128)}, f32[16,5,32]{2,1,0:T(8,128)S(1)}, ...), condition=%wide.region_1.2_spmd.clone, body=%wide.region_0.1_spmd.clone.sunk | while | flops 12803 | bytes 125947 | solution.py:75
  359.0 2.9 copy.781
  366.0 4.9 while.119
  370.9 15.5 %while.117 = (s32[]{:T(128)}, f32[5,2,2]{1,2,0:T(2,128)S(1)}, f32[16,5,2,2]{1,3,2,0:T(2,128)}, s32[]{:T(128)}, s32[]{:T(128)}) while((s32[]{:T(128)}, f32[5,2,2]{1,2,0:T(2,128)S(1)}, f32[16,5,2,2]{1,3,2,0:T(2,128)}, s32[]{:T(128)}, s32[]{:T(128)}) %tuple.729), condition=%wide.region_7.8_spmd, body=%wide.region_6.7_spmd.sunk | while | flops 483 | bytes 805 | solution.py:122
  395.2 277.0 %while.120 = (s32[]{:T(128)}, f32[5]{0:T(128)}, f32[5,128]{1,0:T(8,128)S(1)}, f32[3,32,5]{1,0,2:T(4,128)}, f32[3,32,5,128]{3,2,1,0:T(8,128)}, /*index=5*/f32[3,3...) while((s32[]{:T(128)}, f32[5]{0:T(128)}, ...), condition=%wide.region_15.16_spmd, body=%wide.region_14.15_spmd.sunk | while | flops 92823 | bytes 722685 | solution.py:147
  672.2 1.8 constant_dynamic-update-slice_fusion.95
  679.1 1.9 multiply_subtract_fusion
  693.9 3.4 copy.765
  697.4 3.4 copy.762
  702.6 36.8 %all_gather.20 = f32[16,5,2,2]{1,3,2,0:T(2,128)S(1)} all-gather(f32[1,5,2,2]{1,3,2,0:T(2,128)S(1)} %copy-done.42), channel_id=1, replica_groups=mesh['azim'=16,'rad'=8,'axial'=2] {'azim'}, dimensions={0}, use_global_device_ids=true | all-gather | bytes 1360 | tf_op jit(solution)/shard_map/all_gather | solution.py:13
  739.4 3.7 copy.770
  743.1 3.6 copy.768
  746.7 3.9 fusion.358
  751.0 2.8 fusion.361
  762.2 73.5 %all-gather.5.cloned.1.call-done = f32[80,2,16,128]{3,2,1,0:T(8,128)} async-done(((f32[5,2,16,128]{3,2,1,0:T(8,128)}), f32[80,2,16,128]{3,2,1,0:T(8,128)}) %all-gather.5.cloned.1.call-update) | async-done | bytes 1310736 | tf_op jit(solution)/shard_map/all_gather | solution.py:13
  837.5 171.1 %all-reduce.4.cloned.1.call-done = f32[5,2,16,128]{3,1,2,0:T(2,128)} async-done(((f32[5,2,16,128]{3,1,2,0:T(2,128)}), f32[5,2,16,128]{3,1,2,0:T(2,128)}) %all-reduce.4.cloned.1.call-update) | async-done | bytes 81936 | tf_op jit(solution)/shard_map/psum | solution.py:27
  1010.3 2.3 convolution_add_fusion.3
  1012.6 3.1 rev.16
  1016.0 2.6 fusion.363
  1042.0 29.1 %all_gather.23 = f32[16,5,2,2]{1,3,2,0:T(2,128)S(1)} all-gather(f32[1,5,2,2]{1,3,2,0:T(2,128)S(1)} %fusion.424), channel_id=1, replica_groups=mesh['azim'=16,'rad'=8,'axial'=2] {'azim'}, dimensions={0}, use_global_device_ids=true | all-gather | bytes 1360 | tf_op jit(solution)/shard_map/all_gather | solution.py:13
  1071.3 31.2 %all-gather.7.cloned.1.call-done = f32[80,2,16,128]{3,2,1,0:T(8,128)} async-done(((f32[5,2,16,128]{3,2,1,0:T(8,128)}), f32[80,2,16,128]{3,2,1,0:T(8,128)}) %all-gather.7.cloned.1.call-update) | async-done | bytes 1310736 | tf_op jit(solution)/shard_map/all_gather | solution.py:13
  1102.5 26.0 %while.118 = (s32[]{:T(128)}, f32[5,2,2]{2,1,0:T(2,128)S(1)}, f32[5,2,16,128]{3,1,2,0:T(2,128)S(1)}, s32[]{:T(128)}, f32[16,5,2,2]{1,3,2,0:T(2,128)S(1)}, /*inde...) while((s32[]{:T(128)}, f32[5,2,2]{2,1,0:T(2,128)S(1)}, ...), condition=%wide.region_10.11_spmd, body=%wide.region_9.10_spmd.sunk | while | flops 512486 | bytes 574643 | solution.py:22
  1129.6 143.9 %all-reduce.6.cloned.1.call-done = f32[5,2,16,128]{3,1,2,0:T(2,128)} async-done(((f32[5,2,16,128]{3,1,2,0:T(2,128)}), f32[5,2,16,128]{3,1,2,0:T(2,128)}) %all-reduce.6.cloned.1.call-update) | async-done | bytes 81936 | tf_op jit(solution)/shard_map/psum | solution.py:27
  1275.2 2.3 convolution_add_fusion.2
  1277.5 2.2 rev.17
  1279.8 1.8 copy.789
  1281.6 16.4 %all-to-all-start = ((f32[5,32,16,128]{3,2,0,1:T(8,128)}), f32[5,32,16,128]{3,2,0,1:T(8,128)S(1)}, u32[]{:S(2)}, u32[]{:S(2)}) async-start(f32[5,32,16,128]{3,2,0,1:T(8,128)} %copy.789), calls=%async_computation | async-start | bytes 2621440 | tf_op jit(solution)/shard_map/all_to_all | solution.py:169
  1298.7 6.3 while.121
  1311.2 4.6 all-to-all-done
  1316.4 2.2 convolution_bitcast_fusion.2
  1320.1 22.2 %all_to_all.36 = f32[5,4,128,128]{3,1,0,2:T(4,128)S(1)} all-to-all(f32[5,4,128,128]{3,1,0,2:T(4,128)} %copy.864), channel_id=1, replica_groups=mesh['azim'=16,'rad'=8,'axial'=2] {'rad'}, dimensions={2} | all-to-all | bytes 2621440 | tf_op jit(solution)/shard_map/all_to_all | solution.py:165
  (1447 shorter events, 699.1 us)
Async XLA Ops:
  6.5 829.1 %all-gather.5.cloned.1.call-start = ((), (), s32[]{:S(2)}) async-start(), calls=%async_computation.4 | async-start | bytes 1392640 | tf_op jit(solution)/shard_map/all_gather | solution.py:13
  16.6 722.8 %collective-permute-start.1 = (f32[5,32,16,1]{1,2,3,0:T(8,128)}, f32[5,32,16,1]{1,2,3,0:T(8,128)}, u32[]{:S(2)}, u32[]{:S(2)}) collective-permute-start(f32[5,32,16,1]{1,2,3,0:T(8,128)} %copy.769), channel_id=1, source_target_pairs={{0,1},{2,3},{4,5},{6,7},{8,9},{10,11},{12,13},{14,15},{16,17},{18,... | collective-permute-start | bytes 30728 | tf_op jit(solution)/shard_map/ppermute | solution.py:38
  24.2 718.8 %collective-permute-start = (f32[5,32,16,1]{1,2,3,0:T(8,128)}, f32[5,32,16,1]{1,2,3,0:T(8,128)}, u32[]{:S(2)}, u32[]{:S(2)}) collective-permute-start(f32[5,32,16,1]{1,2,3,0:T(8,128)} %copy.767), channel_id=1, source_target_pairs={{1,0},{3,2},{5,4},{7,6},{9,8},{11,10},{13,12},{15,14},{17,16},{19,... | collective-permute-start | bytes 30728 | tf_op jit(solution)/shard_map/ppermute | solution.py:40
  361.9 25.3 %copy-start.33 = (f32[5,512]{1,0:T(8,128)S(1)}, f32[5,512]{1,0:T(8,128)}, u32[]{:S(2)}) copy-start(f32[5,512]{1,0:T(8,128)} %subtract_sqrt_fusion) | copy-start | bytes 30724
  365.6 29.6 %copy-start.14 = (f32[16,5,1,2]{1,3,2,0:T(2,128)}, f32[16,5,1,2]{1,3,2,0:T(2,128)S(1)}, u32[]{:S(2)}) copy-start(f32[16,5,1,2]{1,3,2,0:T(2,128)S(1)} %copy.912) | copy-start | bytes 1924
  365.9 29.2 %copy-start.15 = (f32[16,5,1,2]{1,3,2,0:T(2,128)}, f32[16,5,1,2]{1,3,2,0:T(2,128)S(1)}, u32[]{:S(2)}) copy-start(f32[16,5,1,2]{1,3,2,0:T(2,128)S(1)} %copy.911) | copy-start | bytes 1924
  402.6 40.3 %copy-start.23 = (f32[5]{0:T(128)}, f32[5]{0:T(128)S(1)}, u32[]{:S(2)}) copy-start(f32[5]{0:T(128)S(1)} %get-tuple-element.1869) | copy-start | bytes 64 | tf_op jit(solution)/shard_map/vmap()/while
  404.1 38.8 %copy-start.24 = (f32[5]{0:T(128)}, f32[5]{0:T(128)S(1)}, u32[]{:S(2)}) copy-start(f32[5]{0:T(128)S(1)} %get-tuple-element.1870) | copy-start | bytes 64 | tf_op jit(solution)/shard_map/vmap()/while
  405.6 37.3 %copy-start.25 = (f32[5]{0:T(128)}, f32[5]{0:T(128)S(1)}, u32[]{:S(2)}) copy-start(f32[5]{0:T(128)S(1)} %get-tuple-element.1871) | copy-start | bytes 64 | tf_op jit(solution)/shard_map/vmap()/while
  407.0 35.9 %copy-start.26 = (f32[5]{0:T(128)}, f32[5]{0:T(128)S(1)}, u32[]{:S(2)}) copy-start(f32[5]{0:T(128)S(1)} %get-tuple-element.1872) | copy-start | bytes 64 | tf_op jit(solution)/shard_map/vmap()/while
  408.4 34.5 %copy-start.27 = (f32[5]{0:T(128)}, f32[5]{0:T(128)S(1)}, u32[]{:S(2)}) copy-start(f32[5]{0:T(128)S(1)} %get-tuple-element.1873) | copy-start | bytes 64 | tf_op jit(solution)/shard_map/vmap()/while
  409.8 33.1 %copy-start.28 = (f32[5]{0:T(128)}, f32[5]{0:T(128)S(1)}, u32[]{:S(2)}) copy-start(f32[5]{0:T(128)S(1)} %get-tuple-element.1874) | copy-start | bytes 64 | tf_op jit(solution)/shard_map/vmap()/while
  411.1 31.9 %copy-start.29 = (f32[5]{0:T(128)}, f32[5]{0:T(128)S(1)}, u32[]{:S(2)}) copy-start(f32[5]{0:T(128)S(1)} %get-tuple-element.1875) | copy-start | bytes 64 | tf_op jit(solution)/shard_map/vmap()/while
  412.4 30.5 %copy-start.30 = (f32[5]{0:T(128)}, f32[5]{0:T(128)S(1)}, u32[]{:S(2)}) copy-start(f32[5]{0:T(128)S(1)} %get-tuple-element.1876) | copy-start | bytes 64 | tf_op jit(solution)/shard_map/vmap()/while
  413.8 29.1 %copy-start.31 = (f32[5]{0:T(128)}, f32[5]{0:T(128)S(1)}, u32[]{:S(2)}) copy-start(f32[5]{0:T(128)S(1)} %get-tuple-element.1877) | copy-start | bytes 64 | tf_op jit(solution)/shard_map/vmap()/while
  415.2 27.8 %copy-start.32 = (f32[5]{0:T(128)}, f32[5]{0:T(128)S(1)}, u32[]{:S(2)}) copy-start(f32[5]{0:T(128)S(1)} %get-tuple-element.1878) | copy-start | bytes 64 | tf_op jit(solution)/shard_map/vmap()/while
  416.6 26.3 %copy-start.17 = (f32[5]{0:T(128)}, f32[5]{0:T(128)S(1)}, u32[]{:S(2)}) copy-start(f32[5]{0:T(128)S(1)} %get-tuple-element.1883) | copy-start | bytes 64 | tf_op jit(solution)/shard_map/vmap()/while
  418.9 24.1 %copy-start.18 = (f32[5]{0:T(128)}, f32[5]{0:T(128)S(1)}, u32[]{:S(2)}) copy-start(f32[5]{0:T(128)S(1)} %get-tuple-element.1973) | copy-start | bytes 64 | tf_op jit(solution)/shard_map/vmap()/while
  495.2 39.8 %copy-start.23 = (f32[5]{0:T(128)}, f32[5]{0:T(128)S(1)}, u32[]{:S(2)}) copy-start(f32[5]{0:T(128)S(1)} %get-tuple-element.1869) | copy-start | bytes 64 | tf_op jit(solution)/shard_map/vmap()/while
  496.6 38.4 %copy-start.24 = (f32[5]{0:T(128)}, f32[5]{0:T(128)S(1)}, u32[]{:S(2)}) copy-start(f32[5]{0:T(128)S(1)} %get-tuple-element.1870) | copy-start | bytes 64 | tf_op jit(solution)/shard_map/vmap()/while
  497.9 37.1 %copy-start.25 = (f32[5]{0:T(128)}, f32[5]{0:T(128)S(1)}, u32[]{:S(2)}) copy-start(f32[5]{0:T(128)S(1)} %get-tuple-element.1871) | copy-start | bytes 64 | tf_op jit(solution)/shard_map/vmap()/while
  499.2 35.8 %copy-start.26 = (f32[5]{0:T(128)}, f32[5]{0:T(128)S(1)}, u32[]{:S(2)}) copy-start(f32[5]{0:T(128)S(1)} %get-tuple-element.1872) | copy-start | bytes 64 | tf_op jit(solution)/shard_map/vmap()/while
  500.6 34.5 %copy-start.27 = (f32[5]{0:T(128)}, f32[5]{0:T(128)S(1)}, u32[]{:S(2)}) copy-start(f32[5]{0:T(128)S(1)} %get-tuple-element.1873) | copy-start | bytes 64 | tf_op jit(solution)/shard_map/vmap()/while
  502.0 33.1 %copy-start.28 = (f32[5]{0:T(128)}, f32[5]{0:T(128)S(1)}, u32[]{:S(2)}) copy-start(f32[5]{0:T(128)S(1)} %get-tuple-element.1874) | copy-start | bytes 64 | tf_op jit(solution)/shard_map/vmap()/while
  503.3 31.8 %copy-start.29 = (f32[5]{0:T(128)}, f32[5]{0:T(128)S(1)}, u32[]{:S(2)}) copy-start(f32[5]{0:T(128)S(1)} %get-tuple-element.1875) | copy-start | bytes 64 | tf_op jit(solution)/shard_map/vmap()/while
  504.6 30.4 %copy-start.30 = (f32[5]{0:T(128)}, f32[5]{0:T(128)S(1)}, u32[]{:S(2)}) copy-start(f32[5]{0:T(128)S(1)} %get-tuple-element.1876) | copy-start | bytes 64 | tf_op jit(solution)/shard_map/vmap()/while
  506.0 29.1 %copy-start.31 = (f32[5]{0:T(128)}, f32[5]{0:T(128)S(1)}, u32[]{:S(2)}) copy-start(f32[5]{0:T(128)S(1)} %get-tuple-element.1877) | copy-start | bytes 64 | tf_op jit(solution)/shard_map/vmap()/while
  507.4 27.7 %copy-start.32 = (f32[5]{0:T(128)}, f32[5]{0:T(128)S(1)}, u32[]{:S(2)}) copy-start(f32[5]{0:T(128)S(1)} %get-tuple-element.1878) | copy-start | bytes 64 | tf_op jit(solution)/shard_map/vmap()/while
  508.8 26.3 %copy-start.17 = (f32[5]{0:T(128)}, f32[5]{0:T(128)S(1)}, u32[]{:S(2)}) copy-start(f32[5]{0:T(128)S(1)} %get-tuple-element.1883) | copy-start | bytes 64 | tf_op jit(solution)/shard_map/vmap()/while
  511.1 24.1 %copy-start.18 = (f32[5]{0:T(128)}, f32[5]{0:T(128)S(1)}, u32[]{:S(2)}) copy-start(f32[5]{0:T(128)S(1)} %get-tuple-element.1973) | copy-start | bytes 64 | tf_op jit(solution)/shard_map/vmap()/while
  587.4 39.8 %copy-start.23 = (f32[5]{0:T(128)}, f32[5]{0:T(128)S(1)}, u32[]{:S(2)}) copy-start(f32[5]{0:T(128)S(1)} %get-tuple-element.1869) | copy-start | bytes 64 | tf_op jit(solution)/shard_map/vmap()/while
  588.8 38.4 %copy-start.24 = (f32[5]{0:T(128)}, f32[5]{0:T(128)S(1)}, u32[]{:S(2)}) copy-start(f32[5]{0:T(128)S(1)} %get-tuple-element.1870) | copy-start | bytes 64 | tf_op jit(solution)/shard_map/vmap()/while
  590.1 37.1 %copy-start.25 = (f32[5]{0:T(128)}, f32[5]{0:T(128)S(1)}, u32[]{:S(2)}) copy-start(f32[5]{0:T(128)S(1)} %get-tuple-element.1871) | copy-start | bytes 64 | tf_op jit(solution)/shard_map/vmap()/while
  591.4 35.8 %copy-start.26 = (f32[5]{0:T(128)}, f32[5]{0:T(128)S(1)}, u32[]{:S(2)}) copy-start(f32[5]{0:T(128)S(1)} %get-tuple-element.1872) | copy-start | bytes 64 | tf_op jit(solution)/shard_map/vmap()/while
  592.8 34.4 %copy-start.27 = (f32[5]{0:T(128)}, f32[5]{0:T(128)S(1)}, u32[]{:S(2)}) copy-start(f32[5]{0:T(128)S(1)} %get-tuple-element.1873) | copy-start | bytes 64 | tf_op jit(solution)/shard_map/vmap()/while
  594.2 33.0 %copy-start.28 = (f32[5]{0:T(128)}, f32[5]{0:T(128)S(1)}, u32[]{:S(2)}) copy-start(f32[5]{0:T(128)S(1)} %get-tuple-element.1874) | copy-start | bytes 64 | tf_op jit(solution)/shard_map/vmap()/while
  595.4 31.8 %copy-start.29 = (f32[5]{0:T(128)}, f32[5]{0:T(128)S(1)}, u32[]{:S(2)}) copy-start(f32[5]{0:T(128)S(1)} %get-tuple-element.1875) | copy-start | bytes 64 | tf_op jit(solution)/shard_map/vmap()/while
  596.8 30.4 %copy-start.30 = (f32[5]{0:T(128)}, f32[5]{0:T(128)S(1)}, u32[]{:S(2)}) copy-start(f32[5]{0:T(128)S(1)} %get-tuple-element.1876) | copy-start | bytes 64 | tf_op jit(solution)/shard_map/vmap()/while
  598.2 29.1 %copy-start.31 = (f32[5]{0:T(128)}, f32[5]{0:T(128)S(1)}, u32[]{:S(2)}) copy-start(f32[5]{0:T(128)S(1)} %get-tuple-element.1877) | copy-start | bytes 64 | tf_op jit(solution)/shard_map/vmap()/while
  599.5 27.7 %copy-start.32 = (f32[5]{0:T(128)}, f32[5]{0:T(128)S(1)}, u32[]{:S(2)}) copy-start(f32[5]{0:T(128)S(1)} %get-tuple-element.1878) | copy-start | bytes 64 | tf_op jit(solution)/shard_map/vmap()/while
  600.9 26.3 %copy-start.17 = (f32[5]{0:T(128)}, f32[5]{0:T(128)S(1)}, u32[]{:S(2)}) copy-start(f32[5]{0:T(128)S(1)} %get-tuple-element.1883) | copy-start | bytes 64 | tf_op jit(solution)/shard_map/vmap()/while
  603.2 24.1 %copy-start.18 = (f32[5]{0:T(128)}, f32[5]{0:T(128)S(1)}, u32[]{:S(2)}) copy-start(f32[5]{0:T(128)S(1)} %get-tuple-element.1973) | copy-start | bytes 64 | tf_op jit(solution)/shard_map/vmap()/while
  754.6 254.0 %all-reduce.4.cloned.1.call-start = ((), (), s32[]{:S(2)}) async-start(), calls=%async_computation.2 | async-start | bytes 163840 | tf_op jit(solution)/shard_map/psum | solution.py:27
  837.4 265.0 %all-gather.7.cloned.1.call-start = ((), (), s32[]{:S(2)}) async-start(), calls=%async_computation.5 | async-start | bytes 1392640 | tf_op jit(solution)/shard_map/all_gather | solution.py:13
  1018.6 22.0 %copy-start.107 = (f32[5]{0:T(128)S(1)}, f32[5]{0:T(128)}, u32[]{:S(2)}) copy-start(f32[5]{0:T(128)} %get-tuple-element.1237) | copy-start | bytes 64
  1018.6 22.1 %copy-start.106 = (f32[5]{0:T(128)S(1)}, f32[5]{0:T(128)}, u32[]{:S(2)}) copy-start(f32[5]{0:T(128)} %get-tuple-element.1235) | copy-start | bytes 64
  1018.6 22.1 %copy-start.105 = (f32[5]{0:T(128)S(1)}, f32[5]{0:T(128)}, u32[]{:S(2)}) copy-start(f32[5]{0:T(128)} %get-tuple-element.1233) | copy-start | bytes 64
  1018.6 22.2 %copy-start.104 = (f32[5]{0:T(128)S(1)}, f32[5]{0:T(128)}, u32[]{:S(2)}) copy-start(f32[5]{0:T(128)} %get-tuple-element.1231) | copy-start | bytes 64
  1018.6 22.3 %copy-start.103 = (f32[5]{0:T(128)S(1)}, f32[5]{0:T(128)}, u32[]{:S(2)}) copy-start(f32[5]{0:T(128)} %get-tuple-element.1229) | copy-start | bytes 64
  1018.7 22.4 %copy-start.102 = (f32[5]{0:T(128)S(1)}, f32[5]{0:T(128)}, u32[]{:S(2)}) copy-start(f32[5]{0:T(128)} %get-tuple-element.1227) | copy-start | bytes 64
  1018.7 22.5 %copy-start.101 = (f32[5]{0:T(128)S(1)}, f32[5]{0:T(128)}, u32[]{:S(2)}) copy-start(f32[5]{0:T(128)} %get-tuple-element.1225) | copy-start | bytes 64
  1018.7 22.6 %copy-start.100 = (f32[5]{0:T(128)S(1)}, f32[5]{0:T(128)}, u32[]{:S(2)}) copy-start(f32[5]{0:T(128)} %get-tuple-element.1223) | copy-start | bytes 64
  1018.7 22.7 %copy-start.99 = (f32[5]{0:T(128)S(1)}, f32[5]{0:T(128)}, u32[]{:S(2)}) copy-start(f32[5]{0:T(128)} %get-tuple-element.1221) | copy-start | bytes 64
  1018.7 22.7 %copy-start.98 = (f32[5]{0:T(128)S(1)}, f32[5]{0:T(128)}, u32[]{:S(2)}) copy-start(f32[5]{0:T(128)} %get-tuple-element.1219) | copy-start | bytes 64
  1018.7 22.8 %copy-start.97 = (f32[5]{0:T(128)S(1)}, f32[5]{0:T(128)}, u32[]{:S(2)}) copy-start(f32[5]{0:T(128)} %get-tuple-element.1217) | copy-start | bytes 64
  1018.7 22.9 %copy-start.96 = (f32[5]{0:T(128)S(1)}, f32[5]{0:T(128)}, u32[]{:S(2)}) copy-start(f32[5]{0:T(128)} %get-tuple-element.1215) | copy-start | bytes 64
  1018.7 52.4 %copy-start.77 = (f32[5]{0:T(128)S(1)}, f32[5]{0:T(128)}, u32[]{:S(2)}) copy-start(f32[5]{0:T(128)} %get-tuple-element.956) | copy-start | bytes 64
  1018.7 52.4 %copy-start.95 = (f32[5]{0:T(128)S(1)}, f32[5]{0:T(128)}, u32[]{:S(2)}) copy-start(f32[5]{0:T(128)} %get-tuple-element.1214) | copy-start | bytes 64
  1019.6 253.9 %all-reduce.6.cloned.1.call-start = ((), (), s32[]{:S(2)}) async-start(), calls=%async_computation.3 | async-start | bytes 163840 | tf_op jit(solution)/shard_map/psum | solution.py:27
  1020.5 50.7 %copy-start.116 = (f32[128]{0:T(128)S(1)}, f32[128]{0:T(128)}, u32[]{:S(2)}) copy-start(f32[128]{0:T(128)} %get-tuple-element.1390) | copy-start | bytes 1540
  1102.4 26.1 %copy-start.75 = (f32[5,2,2,1]{2,1,3,0:T(2,128)S(1)}, f32[5,2,2,1]{2,1,3,0:T(2,128)}, u32[]{:S(2)}) copy-start(f32[5,2,2,1]{2,1,3,0:T(2,128)} %copy.878) | copy-start | bytes 244
  1102.5 27.1 %copy-start.7 = (f32[16,5,32,1]{2,0,3,1:T(8,128)S(1)}, f32[16,5,32,1]{2,0,3,1:T(8,128)}, u32[]{:S(2)}) copy-start(f32[16,5,32,1]{2,0,3,1:T(8,128)} %copy-done.6) | copy-start | bytes 30724
  1102.5 27.1 %copy-start.9 = (f32[16,5,32,1]{2,0,3,1:T(8,128)S(1)}, f32[16,5,32,1]{2,0,3,1:T(8,128)}, u32[]{:S(2)}) copy-start(f32[16,5,32,1]{2,0,3,1:T(8,128)} %copy-done.8) | copy-start | bytes 30724
  1281.6 34.1 %all-to-all-start = ((f32[5,32,16,128]{3,2,0,1:T(8,128)}), f32[5,32,16,128]{3,2,0,1:T(8,128)S(1)}, u32[]{:S(2)}, u32[]{:S(2)}) async-start(f32[5,32,16,128]{3,2,0,1:T(8,128)} %copy.789), calls=%async_computation | async-start | bytes 2621440 | tf_op jit(solution)/shard_map/all_to_all | solution.py:169
  (96 other events, 774.2 us)
Sparse Core Ops, SparseCore 0:
  754.8 80.8 all-gather.4
  838.2 170.3 all-reduce.3
  1019.7 82.6 all-gather.6
  1129.7 143.7 all-reduce.5
where the time goes:
time: 1380 us; the launch traced here: 1350 us
  local copies, waits for them, and re-layouts  468 us (34%)
  waiting for transfers between devices  424 us (31%)
  other arithmetic  295 us (21%)
  blocking collectives  88.1 us (6%)
  matrix products  35.1 us (3%)
  starting transfers between devices  23.2 us (2%)
  between operations  14.8 us (1%)
    psum x2, waiting for transfers between devices, from_root(): return lax.psum(kept, axis)  315 us
    broadcast_in_dim x159, local copies, waits for them, and re-layouts, band_inverse(): return lax.linalg.tridiagonal_solve(below, middle, above, unit)  133 us
    mul x128, local copies, waits for them, and re-layouts, row_step(): second_now[..., None] * prev_two  108 us
    all_gather x2, waiting for transfers between devices, carried_in(): gathered = jax.tree.map(lambda a: lax.all_gather(a, axis), part)  105 us
    dynamic_update_slice x64, other arithmetic, lower_inverse(): _, rows = lax.scan(row_step, (start, start), inputs)  97.2 us
    while x135, other arithmetic  73 us
    all_gather x2, blocking collectives, carried_in(): gathered = jax.tree.map(lambda a: lax.all_gather(a, axis), part)  66 us
    sub x49, other arithmetic, band_inverse(): return lax.linalg.tridiagonal_solve(below, middle, above, unit)  63.3 us
  transfers between devices with their start and end apart: 7, of which 5 were waited for; matrix products, arithmetic and copies ran while one was open for 53% of the time, Pallas kernels for 0%

commit v1 on v0

v1 whole, which is shorter than its diff:
```python
import jax
import jax.numpy as jnp
from jax import lax
from jax.experimental import pallas as pl
from jax.experimental.pallas import tpu as pltpu
from jax.sharding import PartitionSpec as P

MESH = pl.DeviceIdType.MESH
F = 5
NA, NR, NX = 16, 8, 2
CA, CR, LX = 32, 16, 128
G = CA // NR
QA = 24
QR = 2 * F * G
f32 = jnp.float32


def lane_bcast(column, rows):
    return jnp.broadcast_to(column, (rows, LX))


def body(
    res_hbm, lv, dis, azc, rdc, out_hbm,
    x, obuf, xr, hs, hr, ct, cw, rt, rep, tab, traj, ktab, mt, rtraj, rtab, rmt,
    s1, r1, s2, r2, s3, r3, s4, r4,
    in_sem, out_sem, hsem, ss1, rs1, ss2, rs2, ss3, rs3, ss4, rs4,
):
    ia, ir, ix = lax.axis_index("azim"), lax.axis_index("rad"), lax.axis_index("axial")

    def azim_peer(d):
        return lax.rem(ia + d, NA)

    def rad_peer(d):
        return lax.rem(ir + d, NR)

    barrier = pltpu.get_barrier_semaphore()
    pl.semaphore_signal(barrier, inc=1, device_id={"axial": 1 - ix}, device_id_type=MESH)
    for d in range(1, NA):
        pl.semaphore_signal(barrier, inc=1, device_id={"azim": azim_peer(d)}, device_id_type=MESH)
    for d in range(1, NR):
        pl.semaphore_signal(barrier, inc=1, device_id={"rad": rad_peer(d)}, device_id_type=MESH)
    load = pltpu.make_async_copy(res_hbm, x, in_sem)
    load.start()

    pad = jnp.zeros((8 - F, NA * CA), f32)
    for c in range(4):
        ct[c] = jnp.transpose(jnp.concatenate([azc[c], pad], axis=0))
    cw[0] = jnp.sqrt(1.0 - (ct[0] + ct[1]) * (ct[0] + ct[1]))
    cw[1] = jnp.sqrt(1.0 - (ct[2] + ct[3]) * (ct[2] + ct[3]))
    mine = pl.ds(pl.multiple_of(ia * CA, CA), CA)
    for c in range(6):
        own = ct[c, mine] if c < 4 else cw[c - 4, mine]
        for f in range(F):
            tab[c, f] = lane_bcast(own[:, f : f + 1], CA)

    lane = lax.broadcasted_iota(jnp.int32, (CR, LX), 1)
    edge = (LX - 1) * (1 - ix)
    load.wait()

    def pack(i, held):
        first, second = held
        for k in range(4):
            a = i * 4 + k
            for f in range(F):
                place = 32 * (f % 4) + a
                turned = pltpu.roll(x[f, a], lax.rem(place + LX - edge, LX), 1)
                if f < 4:
                    first = jnp.where(lane == place, turned, first)
                else:
                    second = jnp.where(lane == place, turned, second)
        return first, second

    zero = jnp.zeros((CR, LX), f32)
    first, second = lax.fori_loop(0, CA // 4, pack, (zero, zero))
    hs[0:CR] = first
    hs[CR : 2 * CR] = second

    pl.semaphore_wait(barrier, NA + NR - 1)
    halo = pltpu.make_async_remote_copy(
        src_ref=hs, dst_ref=hr, send_sem=hsem.at[0], recv_sem=hsem.at[1],
        device_id={"axial": 1 - ix}, device_id_type=MESH,
    )
    halo.start()

    not_low = (lane != 0).astype(f32)
    not_high = (lane != LX - 1).astype(f32)

    def mix(i, _):
        for k in range(2):
            a = i * 2 + k
            old = [x[f, a] for f in range(F)]
            for g in range(F):
                c = lv[g, 0] * old[0]
                for f in range(1, F):
                    c = c + lv[g, f] * old[f]
                near = pltpu.roll(c, 1, 1) * not_low + pltpu.roll(c, LX - 1, 1) * not_high
                x[g, a] = c + dis[g] * (near - 2.0 * c)
        return 0

    lax.fori_loop(0, CA // 2, mix, 0)
    halo.wait()
    at_edge = (lane == edge).astype(f32)
    far = [pltpu.roll(hr[0:CR], (LX - 32 * f) % LX, 1) for f in range(4)] + [hr[CR : 2 * CR]]
    side = []
    for g in range(F):
        c = lv[g, 0] * far[0]
        for f in range(1, F):
            c = c + lv[g, f] * far[f]
        side.append(dis[g] * c)

    def row(ref, c, f, j):
        return jnp.broadcast_to(ref[c, f, pl.ds(j, 1), :], (CR, LX))

    def lower(i, state):
        one, two = list(state[:F]), list(state[F:])
        for k in range(4):
            j = i * 4 + k
            for f in range(F):
                here = x[f, j] + pltpu.roll(side[f], lax.rem(edge + LX - j, LX), 1) * at_edge
                now = row(tab, 4, f, j) * here + row(tab, 1, f, j) * two[f] + row(tab, 0, f, j) * one[f]
                x[f, j] = now
                one[f], two[f] = now, one[f]
        return tuple(one) + tuple(two)

    def upper(i, state):
        one, two = list(state[:F]), list(state[F:])
        for k in range(4):
            j = CA - 1 - (i * 4 + k)
            for f in range(F):
                now = row(tab, 5, f, j) * x[f, j] + row(tab, 3, f, j) * two[f] + row(tab, 2, f, j) * one[f]
                x[f, j] = now
                one[f], two[f] = now, one[f]
        return tuple(one) + tuple(two)

    nothing = (zero,) * (2 * F)
    low = lax.fori_loop(0, CA // 4, lower, nothing)
    high = lax.fori_loop(0, CA // 4, upper, nothing)
    leaving = list(low) + list(high)
    for v in range(4):
        for f in range(F):
            s1[pl.ds(v * F + f, NA, stride=QA), :] = leaving[v * F + f]
    for n in range(4 * F, QA):
        s1[pl.ds(n, NA, stride=QA), :] = zero

    def span(i, size):
        return pl.ds(pl.multiple_of(i * size, 8), size)

    def exchange(src, dst, ssem, rsem, axis, peer, me, size):
        return pltpu.make_async_remote_copy(
            src_ref=src.at[span(peer, size)], dst_ref=dst.at[span(me, size)],
            send_sem=ssem.at[peer], recv_sem=rsem.at[me],
            device_id={axis: peer}, device_id_type=MESH,
        )

    def send_all(src, dst, ssem, rsem, axis):
        n, me, size = (NA, ia, QA) if axis == "azim" else (NR, ir, QR)
        for d in range(1, n):
            exchange(src, dst, ssem, rsem, axis, lax.rem(me + d, n), me, size).start()
        dst[span(me, size)] = src[span(me, size)]

    def receive_all(src, dst, ssem, rsem, axis):
        n, me, size = (NA, ia, QA) if axis == "azim" else (NR, ir, QR)
        for d in range(1, n):
            peer = lax.rem(me + d, n)
            pltpu.make_async_remote_copy(
                src_ref=src.at[span(peer, size)], dst_ref=dst.at[span(peer, size)],
                send_sem=ssem.at[peer], recv_sem=rsem.at[peer],
                device_id={axis: peer}, device_id_type=MESH,
            ).wait()

    send_all(s1, r1, ss1, rs1, "azim")

    nil, unit = jnp.zeros((NA, 8), f32), jnp.ones((NA, 8), f32)

    def step_rows(ref, c, j):
        return ref[c, pl.ds(j, NA, stride=CA), :]

    first_low, second_low = [(unit, nil), (nil, unit)], []
    path = []
    for e in range(2):
        one, two = first_low[e]
        steps = []
        for j in range(CA):
            now = step_rows(ct, 0, j) * one + step_rows(ct, 1, j) * two
            steps.append(now)
            one, two = now, one
        path.append(steps)
    maps = [path[0][CA - 1], path[1][CA - 1], path[0][CA - 2], path[1][CA - 2]]
    cross, turn = [], []
    for e in range(4):
        one, two = [(nil, nil), (nil, nil), (unit, nil), (nil, unit)][e]
        for j in range(CA - 1, -1, -1):
            now = step_rows(ct, 2, j) * one + step_rows(ct, 3, j) * two
            if e < 2:
                now = now + step_rows(cw, 1, j) * path[e][j]
            traj[e, j * NA : (j + 1) * NA] = now
            one, two = now, one
        (cross if e < 2 else turn).append((one, two))
    maps += [cross[0][0], cross[1][0], cross[0][1], cross[1][1]]
    maps += [turn[0][0], turn[1][0], turn[0][1], turn[1][1]]
    maps = [jnp.transpose(m) for m in maps]
    M, X, N = maps[0:4], maps[4:8], maps[8:12]

    def column(m, k):
        return lane_bcast(m[:, k : k + 1], 8)

    def times(p, q):
        return [
            p[0] * q[0] + p[1] * q[2], p[0] * q[1] + p[1] * q[3],
            p[2] * q[0] + p[3] * q[2], p[2] * q[1] + p[3] * q[3],
        ]

    def closing(total):
        a, b, c, d = 1.0 - total[0], -total[1], -total[2], 1.0 - total[3]
        inverse = 1.0 / (a * d - b * c)
        return [d * inverse, -b * inverse, -c * inverse, a * inverse]

    for k in range(NA):
        for n in range(12):
            mt[n, k] = column(maps[n], k)
    ones, zeros = jnp.ones((8, LX), f32), jnp.zeros((8, LX), f32)
    run = [ones, zeros, zeros, ones]
    for k in range(NA):
        for n in range(4):
            mt[12 + n, k] = run[n]
        run = times([mt[n, k] for n in range(4)], run)
    close_low = closing(run)
    run = [ones, zeros, zeros, ones]
    for k in range(NA - 1, -1, -1):
        for n in range(4):
            mt[16 + n, k] = run[n]
        run = times([mt[8 + n, k] for n in range(4)], run)
    close_high = closing(run)
    for e in range(4):
        own = traj[e, pl.ds(ia, CA, stride=NA), :]
        for f in range(F):
            ktab[e, f] = lane_bcast(own[:, f : f + 1], CA)

    for c in range(2):
        for f in range(F):
            rep[c, f * G : (f + 1) * G] = jnp.broadcast_to(rdc[c, f : f + 1, :], (G, LX))
        rep[c, F * G :] = jnp.zeros((24 - F * G, LX), f32)
        rt[c] = jnp.transpose(rep[c])
    keep = jnp.ones((NR, 24), f32)
    lead = keep
    ys, cs = [], []
    for i in range(CR):
        l = rt[0, pl.ds(i, NR, stride=CR), :]
        u = rt[1, pl.ds(i, NR, stride=CR), :]
        s = 1.0 + l * keep
        r = 1.0 / (s + u)
        keep = s * r
        c = u * r
        la = l * r
        lead = la * lead
        ys.append(lead)
        cs.append(c)
        rtraj[0, i * NR : (i + 1) * NR] = jnp.sqrt(jnp.sqrt(1.0 + l + u)) * r
        rtraj[1, i * NR : (i + 1) * NR] = la
        rtraj[2, i * NR : (i + 1) * NR] = c
    left, right = jnp.zeros((NR, 24), f32), jnp.ones((NR, 24), f32)
    lefts, rights = [None] * CR, [None] * CR
    for i in range(CR - 1, -1, -1):
        left = ys[i] + cs[i] * left
        right = cs[i] * right
        lefts[i], rights[i] = left, right
        rtraj[3, i * NR : (i + 1) * NR] = left
        rtraj[4, i * NR : (i + 1) * NR] = right
    for e in range(5):
        own = rtraj[e, pl.ds(ir, CR, stride=NR), :]
        for f in range(F):
            rtab[e, f] = lane_bcast(own[:, f * G : f * G + 1], CR)
    ends = [jnp.transpose(m) for m in (lefts[0], rights[0], lefts[CR - 1], rights[CR - 1])]
    beta = jnp.zeros((24, LX), f32)
    for k in range(NR):
        l0, r0, l1, rr1 = [lane_bcast(m[:, k : k + 1], 24) for m in ends]
        gamma = 1.0 / (1.0 - l0 * beta)
        h = gamma * r0
        rmt[0, k], rmt[1, k], rmt[2, k], rmt[3, k] = l0, l1, gamma, h
        beta = rr1 + l1 * beta * h
        rmt[4, k] = beta

    receive_all(s1, r1, ss1, rs1, "azim")

    def part(k, v):
        return r1[pl.ds(k * QA + v * F, 8), :]

    def apply(m, k, one, two):
        return (mt[m, k] * one + mt[m + 1, k] * two, mt[m + 2, k] * one + mt[m + 3, k] * two)

    def through(m, one, two):
        return (m[0] * one + m[1] * two, m[2] * one + m[3] * two)

    one, two = zeros, zeros
    entering = []
    for k in range(NA):
        entering.append((one, two))
        p, q = apply(0, k, one, two)
        one, two = p + part(k, 0), q + part(k, 1)
    start = through(close_low, one, two)
    above = []
    for k in range(NA):
        p, q = apply(12, k, *start)
        p, q = entering[k][0] + p, entering[k][1] + q
        s2[pl.ds(k * QA, F), :] = p[0:F]
        s2[pl.ds(k * QA + F, F), :] = q[0:F]
        c, d = apply(4, k, p, q)
        above.append((c + part(k, 2), d + part(k, 3)))
    one, two = zeros, zeros
    for k in range(NA - 1, -1, -1):
        entering[k] = (one, two)
        p, q = apply(8, k, one, two)
        one, two = p + above[k][0], q + above[k][1]
    start = through(close_high, one, two)
    for k in range(NA):
        p, q = apply(16, k, *start)
        p, q = entering[k][0] + p, entering[k][1] + q
        s2[pl.ds(k * QA + 2 * F, F), :] = p[0:F]
        s2[pl.ds(k * QA + 3 * F, F), :] = q[0:F]
        s2[pl.ds(k * QA + 4 * F, QA - 4 * F), :] = zeros[0 : QA - 4 * F]

    send_all(s2, r2, ss2, rs2, "azim")
    receive_all(s2, r2, ss2, rs2, "azim")

    for f in range(F):
        enter = [r2[pl.ds(v * F + f, NA, stride=QA), :] for v in range(4)]

        def correct(i, _):
            for k in range(4):
                j = i * 4 + k
                at = pl.ds(pl.multiple_of((f * CA + j) * CR, CR), CR)
                total = x[f, j] + row(ktab, 0, f, j) * enter[0] + row(ktab, 1, f, j) * enter[1]
                xr[at, :] = total + row(ktab, 2, f, j) * enter[2] + row(ktab, 3, f, j) * enter[3]
            return 0

        lax.fori_loop(0, CA // 4, correct, 0)

    def rrow(e, f, i):
        return jnp.broadcast_to(rtab[e, f, pl.ds(i, 1), :], (8, LX))

    for f in range(F):
        ys = [[None] * CR for _ in range(G)]
        for g in range(G):
            y = None
            for i in range(CR):
                v = xr[pl.ds((f * CA + g * 8) * CR + i, 8, stride=CR), :] * rrow(0, f, i)
                y = v if y is None else v + rrow(1, f, i) * y
                ys[g][i] = y
            s3[pl.ds(F * G + f * G + g, NR, stride=QR), :] = y
            obuf[f, CR - 1, g * 8 : (g + 1) * 8] = y
            for i in range(CR - 2, -1, -1):
                y = ys[g][i] + rrow(2, f, i) * y
                obuf[f, i, g * 8 : (g + 1) * 8] = y
            s3[pl.ds(f * G + g, NR, stride=QR), :] = y

    send_all(s3, r3, ss3, rs3, "rad")
    receive_all(s3, r3, ss3, rs3, "rad")

    n = F * G
    alpha = jnp.zeros((n, LX), f32)
    gs, alphas = [], []
    for k in range(NR):
        first = r3[pl.ds(k * QR, n), :]
        last = r3[pl.ds(k * QR + n, n), :]
        g = rmt[2, k, 0:n] * (first + rmt[0, k, 0:n] * alpha)
        if k == 0:
            alpha = last
        else:
            alpha = last + rmt[1, k, 0:n] * (alpha + rmt[4, k - 1, 0:n] * g)
        gs.append(g)
        alphas.append(alpha)
    after = jnp.zeros((n, LX), f32)
    s4[pl.ds(0, n), :] = after
    for k in range(NR - 1, -1, -1):
        s4[pl.ds(k * QR + n, n), :] = after
        if k + 1 < NR:
            s4[pl.ds((k + 1) * QR, n), :] = alphas[k] + rmt[4, k, 0:n] * after
        after = gs[k] + rmt[3, k, 0:n] * after

    send_all(s4, r4, ss4, rs4, "rad")
    receive_all(s4, r4, ss4, rs4, "rad")

    stores = []
    for f in range(F):
        for g in range(G):
            before = r4[pl.ds(f * G + g, NR, stride=QR), :]
            behind = r4[pl.ds(n + f * G + g, NR, stride=QR), :]
            for i in range(CR):
                v = obuf[f, i, g * 8 : (g + 1) * 8] + rrow(3, f, i) * before + rrow(4, f, i) * behind
                xr[pl.ds((f * CA + g * 8) * CR + i, 8, stride=CR), :] = v
        rows = CA * CR
        store = pltpu.make_async_copy(xr.at[pl.ds(f * rows, rows)], out_hbm.at[pl.ds(f * rows, rows)], out_sem.at[f])
        store.start()
        stores.append(store)
    for store in stores:
        store.wait()


def local(residual, left_vec, dissip, azim_coef, radial_coef):
    vm = pltpu.VMEM
    dma = pltpu.SemaphoreType.DMA
    smem = pl.BlockSpec(memory_space=pltpu.SMEM)
    whole = pl.BlockSpec(memory_space=pltpu.VMEM)
    out = pl.pallas_call(
        body,
        out_shape=jax.ShapeDtypeStruct((F * CA * CR, LX), f32),
        in_specs=[pl.BlockSpec(memory_space=pl.ANY), smem, smem, whole, whole],
        out_specs=pl.BlockSpec(memory_space=pl.ANY),
        scratch_shapes=[
            vm((F, CA, CR, LX), f32),
            vm((F, CR, CA, LX), f32),
            vm((F * CA * CR, LX), f32),
            vm((2 * CR, LX), f32), vm((2 * CR, LX), f32),
            vm((4, NA * CA, 8), f32), vm((2, NA * CA, 8), f32),
            vm((2, NR * CR, 24), f32), vm((2, 24, NR * CR), f32),
            vm((6, F, CA, LX), f32),
            vm((4, CA * NA, 8), f32),
            vm((4, F, CA, LX), f32),
            vm((20, NA, 8, LX), f32),
            vm((5, CR * NR, 24), f32),
            vm((5, F, CR, LX), f32),
            vm((5, NR, 24, LX), f32),
            vm((NA * QA, LX), f32), vm((NA * QA, LX), f32),
            vm((NA * QA, LX), f32), vm((NA * QA, LX), f32),
            vm((NR * QR, LX), f32), vm((NR * QR, LX), f32),
            vm((NR * QR, LX), f32), vm((NR * QR, LX), f32),
            dma, dma((F,)), dma((2,)),
            dma((NA,)), dma((NA,)), dma((NA,)), dma((NA,)),
            dma((NR,)), dma((NR,)), dma((NR,)), dma((NR,)),
        ],
        compiler_params=pltpu.CompilerParams(
            collective_id=0, has_side_effects=True, vmem_limit_bytes=48 * 1024 * 1024
        ),
        name="adi",
    )(residual, left_vec, dissip, azim_coef, radial_coef)
    return out.reshape(F, CA, CR, LX)


def solution(mesh):
    placed = (P(None, "azim", "rad", "axial"), P(), P(), P(), P())
    return jax.shard_map(
        local,
        mesh=mesh,
        in_specs=placed,
        out_specs=P(None, "azim", "rad", "axial"),
        check_vma=False,
    )
```

time: 1380 us -> 48.9 us (0.04); the launches traced: 1350 us -> 48.7 us
  local copies, waits for them, and re-layouts: 468 us -> 5.2 us
  waiting for transfers between devices: 424 us -> 0 us
  other arithmetic: 295 us -> 0 us
  blocking collectives: 88.1 us -> 0 us
  Pallas kernels: 0 us -> 43.4 us
  matrix products: 35.1 us -> 0 us
  starting transfers between devices: 23.2 us -> 0 us
  between operations: 14.8 us -> 0.02 us
    psum x2 -> x0, waiting for transfers between devices: 315 us -> none  [from_root(): return lax.psum(kept, axis)]
    mul x199 -> x0, local copies, waits for them, and re-layouts: 152 us -> none  [the longest x128 108 us: row_step(): second_now[..., None] * prev_two]
    broadcast_in_dim x163 -> x0, local copies, waits for them, and re-layouts: 133 us -> none  [the longest x159 133 us: band_inverse(): return lax.linalg.tridiagonal_solve(below, middle, above, unit)]
    all_gather x2 -> x0, waiting for transfers between devices: 105 us -> none  [carried_in(): gathered = jax.tree.map(lambda a: lax.all_gather(a, axis), part)]
    dynamic_update_slice x64 -> x0, other arithmetic: 97.2 us -> none  [lower_inverse(): _, rows = lax.scan(row_step, (start, start), inputs)]
    while x135 -> x0, other arithmetic: 73 us -> none
    all_gather x2 -> x0, blocking collectives: 66 us -> none  [carried_in(): gathered = jax.tree.map(lambda a: lax.all_gather(a, axis), part)]
    sub x52 -> x0, other arithmetic: 64.9 us -> none  [the longest x49 63.3 us: band_inverse(): return lax.linalg.tridiagonal_solve(below, middle, above, unit)]
  transfers between devices with their start and end apart: 7 -> 0, of which waited for: 5 -> 0; matrix products, arithmetic and copies ran while one was open for 53% -> 0% of each run, Pallas kernels for 0% -> 0%
where the time goes in v1:
time: 48.9 us; the launch traced here: 48.7 us
  Pallas kernels  43.4 us (89%)
  local copies, waits for them, and re-layouts  5.2 us (11%)
    pallas_call x1, Pallas kernels, local(): pl.pallas_call(body, out_shape=jax.ShapeDtypeStruct((F * CA * CR, LX), f3...  43.4 us
    unnamed x9, local copies, waits for them, and re-layouts  5.2 us

profile of v1, /device:TPU:1, one launch (start us, length us, event | category | flops | bytes accessed | tf_op | source)
XLA Modules:
  0.0 48.7 jit_solution(8674436281502621017)
XLA Ops:
  0.0 0.7 %copy.7.rdc = f32[2,5,128]{2,1,0:T(8,128)S(1)} copy(f32[2,5,128]{2,0,1:T(2,128)} %param.9) | data formatting | bytes 10240 | tf_op args[4]
  0.7 0.8 %copy.6.azc = f32[4,5,512]{2,1,0:T(8,128)S(1)} copy(f32[4,5,512]{2,0,1:T(4,128)} %param.8) | data formatting | bytes 81920 | tf_op args[3]
  1.5 0.0 copy-start
  1.5 1.3 %copy-done = f32[5,32,16,128]{3,2,1,0:T(8,128)S(1)} copy-done((f32[5,32,16,128]{3,2,1,0:T(8,128)S(1)}, f32[5,32,16,128]{3,2,1,0:T(8,128)}, u32[]{:S(2)}) %copy-start) | copy-done | bytes 1310744
  2.8 0.0 copy-start.1
  2.8 0.7 %copy-done.1 = f32[5,5]{1,0:T(8,128)S(1)} copy-done((f32[5,5]{1,0:T(8,128)S(1)}, f32[5,5]{1,0:T(8,128)}, u32[]{:S(2)}) %copy-start.1) | copy-done | bytes 124
  3.5 0.0 copy-start.2
  3.5 0.7 %copy-done.2 = f32[5]{0:T(128)S(1)} copy-done((f32[5]{0:T(128)S(1)}, f32[5]{0:T(128)}, u32[]{:S(2)}) %copy-start.2) | copy-done | bytes 44
  4.2 43.4 %adi.1 = f32[2560,128]{1,0:T(8,128)S(1)} custom-call(f32[5,32,16,128]{3,2,1,0:T(8,128)S(1)} %copy-done, f32[5,5]{1,0:T(8,128)S(1)} %copy-done.1, f32[5]{0:T(128)S(1)} %copy-done.2, f32[4,5,512]{2,1,0:T(8,128)S(1)} %copy.6.azc, f32[2,5,128]{2,1,0:T(8,128)S(1)} %copy.7.rdc), custom_call_target="tpu_custom_call" | custom-call | tf_op jit(solution)/shard_map/adi/pallas_call | solution.py:404
  47.6 1.1 %copy.9 = f32[5,32,16,128]{3,2,1,0:T(8,128)} copy(f32[5,32,16,128]{3,2,1,0:T(8,128)S(1)} %bitcast.1) | data formatting | bytes 2621440
Async XLA Ops:
  1.5 1.3 %copy-start = (f32[5,32,16,128]{3,2,1,0:T(8,128)S(1)}, f32[5,32,16,128]{3,2,1,0:T(8,128)}, u32[]{:S(2)}) copy-start(f32[5,32,16,128]{3,2,1,0:T(8,128)} %res_hbm.1) | copy-start | bytes 3932164
  2.8 0.7 %copy-start.1 = (f32[5,5]{1,0:T(8,128)S(1)}, f32[5,5]{1,0:T(8,128)}, u32[]{:S(2)}) copy-start(f32[5,5]{1,0:T(8,128)} %lv.1) | copy-start | bytes 304
  3.5 0.7 %copy-start.2 = (f32[5]{0:T(128)S(1)}, f32[5]{0:T(128)}, u32[]{:S(2)}) copy-start(f32[5]{0:T(128)} %dis.1) | copy-start | bytes 64

commit v2 on v1

v2 whole, which is shorter than its diff:
```python
import jax
import jax.numpy as jnp
from jax import lax
from jax.experimental import pallas as pl
from jax.experimental.pallas import tpu as pltpu
from jax.sharding import PartitionSpec as P

MESH = pl.DeviceIdType.MESH
F = 5
NA, NR = 16, 8
CA, CR, LX = 32, 16, 128
G = CA // NR
NV = 4
QA = 24
QB = 2 * F * G
QE = 8
f32 = jnp.float32


def lane_bcast(column, rows):
    return jnp.broadcast_to(column, (rows, LX))


def body(
    res_hbm, lv_hbm, dis_hbm, azc_hbm, rdc_hbm, out,
    x, lvs, diss, azv, rdv, cat, own6, hs, hr, es, ee, ct, rt, rep, tab, traj, ktab, mt, rtraj, rtab, rline, rmt,
    s1, r1, s2, r2, sb1, rb1, sb2, rb2, s3, r3, s4, r4, eloc, re,
    in_sem, hsem, ss1, rs1, sse, rse, ss2, rs2, ssb1, rsb1, ssb2, rsb2, ss3, rs3, ss4, rs4,
):
    ia, ir, ix = lax.axis_index("azim"), lax.axis_index("rad"), lax.axis_index("axial")
    other = 1 - ix

    barrier = pltpu.get_barrier_semaphore()
    for d in range(NA - 1, -1, -1):
        peer = lax.rem(ia + d, NA)
        pl.semaphore_signal(barrier, inc=1, device_id={"azim": peer, "axial": other}, device_id_type=MESH)
        if d:
            pl.semaphore_signal(barrier, inc=1, device_id={"azim": peer}, device_id_type=MESH)
    for d in range(1, NR):
        pl.semaphore_signal(barrier, inc=1, device_id={"rad": lax.rem(ir + d, NR)}, device_id_type=MESH)
    loads = [
        pltpu.make_async_copy(src, dst, in_sem.at[n])
        for n, (src, dst) in enumerate(
            [(azc_hbm, azv), (lv_hbm, lvs), (dis_hbm, diss), (res_hbm, x), (rdc_hbm, rdv)]
        )
    ]
    for load in loads:
        load.start()
    lane = lax.broadcasted_iota(jnp.int32, (CR, LX), 1)
    edge = (LX - 1) * (1 - ix)
    not_low = (lane != 0).astype(f32)
    not_high = (lane != LX - 1).astype(f32)
    at_edge = (lane == edge).astype(f32)
    zero = jnp.zeros((CR, LX), f32)

    loads[0].wait()
    for c in range(4):
        for f in range(F):
            cat[c, f : f + 1, :] = azv[f, c : c + 1, :]
        cat[c, F:8, :] = jnp.zeros((8 - F, NA * CA), f32)
    group = pl.ds(pl.multiple_of((ia // 4) * LX, LX), LX)
    back = lax.rem(LX - lax.rem(ia, 4) * CA, LX)
    own = [pltpu.roll(cat[c, :, group], back, 1) for c in range(4)]
    own.append(jnp.sqrt(1.0 - (own[0] + own[1]) * (own[0] + own[1])))
    own.append(jnp.sqrt(1.0 - (own[2] + own[3]) * (own[2] + own[3])))
    for c in range(6):
        own6[c * 8 : (c + 1) * 8] = own[c]
    turned = jnp.transpose(own6[...])[0:CA]
    for c in range(6):
        for f in range(F):
            tab[c, f] = lane_bcast(turned[:, c * 8 + f : c * 8 + f + 1], CA)

    def row(ref, c, f, j):
        return jnp.broadcast_to(ref[c, f, pl.ds(j, 1), :], (CR, LX))

    for load in loads[1:4]:
        load.wait()
    lv = [[lvs[g, f] for f in range(F)] for g in range(F)]
    dis = [diss[f] for f in range(F)]

    def lower(i, state):
        one, two = list(state[:F]), list(state[F:])
        for k in range(4):
            j = i * 4 + k
            old = [x[f, j] for f in range(F)]
            for g in range(F):
                c = lv[g][0] * old[0]
                for f in range(1, F):
                    c = c + lv[g][f] * old[f]
                now = row(tab, 4, g, j) * c + row(tab, 1, g, j) * two[g] + row(tab, 0, g, j) * one[g]
                x[g, j] = now
                one[g], two[g] = now, one[g]
        return tuple(one) + tuple(two)

    def upper(i, state):
        one, two = list(state[:F]), list(state[F:])
        for k in range(4):
            j = CA - 1 - (i * 4 + k)
            for f in range(F):
                now = row(tab, 5, f, j) * x[f, j] + row(tab, 3, f, j) * two[f] + row(tab, 2, f, j) * one[f]
                x[f, j] = now
                one[f], two[f] = now, one[f]
        return tuple(one) + tuple(two)

    nothing = (zero,) * (2 * F)
    low = lax.fori_loop(0, CA // 4, lower, nothing)
    high = lax.fori_loop(0, CA // 4, upper, nothing)

    def damped(v, f):
        near = pltpu.roll(v, 1, 1) * not_low + pltpu.roll(v, LX - 1, 1) * not_high
        return v + dis[f] * (near - 2.0 * v)

    edges = zero
    for n, v in enumerate(list(low) + list(high)):
        edges = jnp.where(lane == n, pltpu.roll(v, lax.rem(n + LX - edge, LX), 1), edges)
        s1[pl.ds(n, NA, stride=QA), :] = damped(v, n % F)
    for n in range(NV * F, QA):
        s1[pl.ds(n, NA, stride=QA), :] = zero
    for o in range(NA):
        es[o] = edges[o : o + 1]

    def span(i, size):
        return pl.ds(pl.multiple_of(i * size, 8), size)

    def copies(src, dst, ssem, rsem, axis, size):
        n, me = (NA, ia) if axis == "azim" else (NR, ir)
        out_going, in_coming = [], []
        for d in range(1, n):
            peer = lax.rem(me + d, n)
            for place, into in ((me, out_going), (peer, in_coming)):
                into.append(
                    pltpu.make_async_remote_copy(
                        src_ref=src.at[span(peer, size)], dst_ref=dst.at[span(place, size)],
                        send_sem=ssem.at[peer], recv_sem=rsem.at[place],
                        device_id={axis: peer}, device_id_type=MESH,
                    )
                )

        def send():
            for copy in out_going:
                copy.start()
            dst[span(me, size)] = src[span(me, size)]

        def receive():
            for copy in in_coming:
                copy.wait_recv()

        def finish():
            for copy in out_going:
                copy.wait_send()

        return send, receive, finish

    edge_out, edge_in = [], []
    for d in range(NA):
        peer = lax.rem(ia + d, NA)
        for place, into in ((ia, edge_out), (peer, edge_in)):
            into.append(
                pltpu.make_async_remote_copy(
                    src_ref=es.at[peer], dst_ref=ee.at[place], send_sem=sse.at[peer], recv_sem=rse.at[place],
                    device_id={"azim": peer, "axial": other}, device_id_type=MESH,
                )
            )
    send1, receive1, finish1 = copies(s1, r1, ss1, rs1, "azim", QA)
    send2, receive2, finish2 = copies(s2, r2, ss2, rs2, "azim", QA)
    sendb1, receiveb1, finishb1 = copies(sb1, rb1, ssb1, rsb1, "rad", QB)
    sendb2, receiveb2, finishb2 = copies(sb2, rb2, ssb2, rsb2, "rad", QB)
    send3, receive3, finish3 = copies(s3, r3, ss3, rs3, "rad", QE)
    send4, receive4, finish4 = copies(s4, r4, ss4, rs4, "rad", QE)

    pl.semaphore_wait(barrier, 2 * NA + NR - 2)
    for copy in edge_out:
        copy.start()
    send1()

    def pack(i, held):
        first, second = held
        for k in range(4):
            a = i * 4 + k
            for f in range(F):
                place = 32 * (f % 4) + a
                moved = pltpu.roll(x[f, a], lax.rem(place + LX - edge, LX), 1)
                if f < 4:
                    first = jnp.where(lane == place, moved, first)
                else:
                    second = jnp.where(lane == place, moved, second)
        return first, second

    first, second = lax.fori_loop(0, CA // 4, pack, (zero, zero))
    hs[0:CR] = first
    hs[CR : 2 * CR] = second
    halo = pltpu.make_async_remote_copy(
        src_ref=hs, dst_ref=hr, send_sem=hsem.at[0], recv_sem=hsem.at[1],
        device_id={"axial": other}, device_id_type=MESH,
    )
    halo.start()

    for c in range(4):
        ct[c] = jnp.transpose(cat[c])
    nil, unit = jnp.zeros((NA, 8), f32), jnp.ones((NA, 8), f32)

    def step_rows(c, j):
        return ct[c, pl.ds(j, NA, stride=CA), :]

    path = []
    for one, two in ((unit, nil), (nil, unit)):
        steps = []
        for j in range(CA):
            now = step_rows(0, j) * one + step_rows(1, j) * two
            steps.append(now)
            one, two = now, one
        path.append(steps)
    maps = [path[0][CA - 1], path[1][CA - 1], path[0][CA - 2], path[1][CA - 2]]
    state = [(nil, nil), (nil, nil), (unit, nil), (nil, unit)]
    for j in range(CA - 1, -1, -1):
        c, e = step_rows(2, j), step_rows(3, j)
        w = jnp.sqrt(1.0 - (c + e) * (c + e))
        for n in range(4):
            one, two = state[n]
            now = c * one + e * two
            if n < 2:
                now = now + w * path[n][j]
            traj[n, j * NA : (j + 1) * NA] = now
            state[n] = (now, one)
    maps += [state[0][0], state[1][0], state[0][1], state[1][1]]
    maps += [state[2][0], state[3][0], state[2][1], state[3][1]]
    maps = [jnp.transpose(m) for m in maps]

    def column(m, k):
        return lane_bcast(m[:, k : k + 1], 8)

    def times(p, q):
        return [
            p[0] * q[0] + p[1] * q[2], p[0] * q[1] + p[1] * q[3],
            p[2] * q[0] + p[3] * q[2], p[2] * q[1] + p[3] * q[3],
        ]

    def closing(total):
        a, b, c, d = 1.0 - total[0], -total[1], -total[2], 1.0 - total[3]
        inverse = 1.0 / (a * d - b * c)
        return [d * inverse, -b * inverse, -c * inverse, a * inverse]

    for k in range(NA):
        for n in range(12):
            mt[n, k] = column(maps[n], k)
    ones, zeros = jnp.ones((8, LX), f32), jnp.zeros((8, LX), f32)
    run = [ones, zeros, zeros, ones]
    for k in range(NA):
        for n in range(4):
            mt[12 + n, k] = run[n]
        run = times([mt[n, k] for n in range(4)], run)
    close_low = closing(run)
    run = [ones, zeros, zeros, ones]
    for k in range(NA - 1, -1, -1):
        for n in range(4):
            mt[16 + n, k] = run[n]
        run = times([mt[8 + n, k] for n in range(4)], run)
    close_high = closing(run)
    for e in range(NV):
        own = traj[e, pl.ds(ia, CA, stride=NA), :]
        for f in range(F):
            ktab[e, f] = lane_bcast(own[:, f : f + 1], CA)

    loads[4].wait()
    for c in range(2):
        for n in range(QA):
            rep[c, n : n + 1, :] = rdv[n % F, c : c + 1, :]
        rt[c] = jnp.transpose(rep[c])
    keep = jnp.ones((NR, QA), f32)
    lead = keep
    ys, cs = [], []
    for i in range(CR):
        l = rt[0, pl.ds(i, NR, stride=CR), :]
        u = rt[1, pl.ds(i, NR, stride=CR), :]
        s = 1.0 + l * keep
        r = 1.0 / (s + u)
        keep = s * r
        c = u * r
        la = l * r
        lead = la * lead
        ys.append(lead)
        cs.append(c)
        rtraj[0, i * NR : (i + 1) * NR] = jnp.sqrt(jnp.sqrt(1.0 + l + u)) * r
        rtraj[1, i * NR : (i + 1) * NR] = la
        rtraj[2, i * NR : (i + 1) * NR] = c
    left, right = jnp.zeros((NR, QA), f32), jnp.ones((NR, QA), f32)
    lefts, rights = [None] * CR, [None] * CR
    for i in range(CR - 1, -1, -1):
        left = ys[i] + cs[i] * left
        right = cs[i] * right
        lefts[i], rights[i] = left, right
        rtraj[3, i * NR : (i + 1) * NR] = left
        rtraj[4, i * NR : (i + 1) * NR] = right
    for e in range(5):
        own = rtraj[e, pl.ds(ir, CR, stride=NR), :]
        for f in range(F):
            rtab[e, f] = lane_bcast(own[:, f : f + 1], CR)
        own = jnp.transpose(own)
        for i in range(CR):
            rline[e, i] = lane_bcast(own[:, i : i + 1], QA)
    ends = [jnp.transpose(m) for m in (lefts[0], rights[0], lefts[CR - 1], rights[CR - 1])]
    beta = jnp.zeros((QA, LX), f32)
    for k in range(NR):
        l0, r0, l1, rr1 = [lane_bcast(m[:, k : k + 1], QA) for m in ends]
        gamma = 1.0 / (1.0 - l0 * beta)
        h = gamma * r0
        beta = rr1 + l1 * beta * h
        for n, m in enumerate((l0, l1, gamma, h, beta)):
            rmt[n, k * QA : (k + 1) * QA] = m

    halo.wait_recv()
    far = [pltpu.roll(hr[0:CR], (LX - 32 * f) % LX, 1) for f in range(4)] + [hr[CR : 2 * CR]]
    side = [dis[f] * far[f] for f in range(F)]

    def dissipate(i, _):
        for k in range(2):
            a = i * 2 + k
            for f in range(F):
                x[f, a] = damped(x[f, a], f) + pltpu.roll(side[f], lax.rem(edge + LX - a, LX), 1) * at_edge
        return 0

    lax.fori_loop(0, CA // 2, dissipate, 0)

    line = lax.broadcasted_iota(jnp.int32, (QA, LX), 0)
    weight = jnp.zeros((QA, LX), f32)
    for n in range(NV * F):
        weight = jnp.where(line == n, dis[n % F], weight)
    weight = jnp.where(lax.broadcasted_iota(jnp.int32, (QA, LX), 1) == edge, weight, 0.0)

    for copy in edge_in:
        copy.wait_recv()
    receive1()
    beyond = jnp.transpose(ee[:, 0, :])[0:QA]
    for k in range(NA):
        at = pl.ds(k * QA, QA)
        r1[at, :] = r1[at, :] + lane_bcast(beyond[:, k : k + 1], QA) * weight

    def part(k, v):
        return r1[pl.ds(k * QA + v * F, 8), :]

    def apply(m, k, one, two):
        return (mt[m, k] * one + mt[m + 1, k] * two, mt[m + 2, k] * one + mt[m + 3, k] * two)

    def through(m, one, two):
        return (m[0] * one + m[1] * two, m[2] * one + m[3] * two)

    one, two = zeros, zeros
    entering = []
    for k in range(NA):
        entering.append((one, two))
        p, q = apply(0, k, one, two)
        one, two = p + part(k, 0), q + part(k, 1)
    start = through(close_low, one, two)
    above = []
    for k in range(NA):
        p, q = apply(12, k, *start)
        p, q = entering[k][0] + p, entering[k][1] + q
        s2[pl.ds(k * QA, F), :] = p[0:F]
        s2[pl.ds(k * QA + F, F), :] = q[0:F]
        c, d = apply(4, k, p, q)
        above.append((c + part(k, 2), d + part(k, 3)))
    one, two = zeros, zeros
    for k in range(NA - 1, -1, -1):
        entering[k] = (one, two)
        p, q = apply(8, k, one, two)
        one, two = p + above[k][0], q + above[k][1]
    start = through(close_high, one, two)
    for k in range(NA):
        p, q = apply(16, k, *start)
        p, q = entering[k][0] + p, entering[k][1] + q
        s2[pl.ds(k * QA + 2 * F, F), :] = p[0:F]
        s2[pl.ds(k * QA + 3 * F, F), :] = q[0:F]
        s2[pl.ds(k * QA + 4 * F, QA - 4 * F), :] = zeros[0 : QA - 4 * F]

    send2()

    def rrow(e, f, i, rows):
        return jnp.broadcast_to(rtab[e, f, pl.ds(i, 1), :], (rows, LX))

    flat = x.reshape(F * CA * CR, LX)
    for f in range(F):
        for g in range(G):
            def cells(i):
                return pl.ds((f * CA + g * 8) * CR + i, 8, stride=CR)

            ys, y = [], None
            for i in range(CR):
                v = flat[cells(i), :] * rrow(0, f, i, 8)
                y = v if y is None else v + rrow(1, f, i, 8) * y
                ys.append(y)
            sb1[pl.ds(F * G + g * F + f, NR, stride=QB), :] = y
            flat[cells(CR - 1), :] = y
            for i in range(CR - 2, -1, -1):
                y = ys[i] + rrow(2, f, i, 8) * y
                flat[cells(i), :] = y
            sb1[pl.ds(g * F + f, NR, stride=QB), :] = y
    sendb1()
    for n in (3, 7):
        s3[pl.ds(n, NR, stride=QE), :] = jnp.zeros((NR, LX), f32)
        s4[pl.ds(n, NR, stride=QE), :] = jnp.zeros((NR, LX), f32)

    def close_radial(src, dst, size, n, place, at):
        alpha = jnp.zeros((n, LX), f32)
        gs, alphas = [], []
        for k in range(NR):
            first = src[pl.ds(k * size, n), :]
            last = src[pl.ds(k * size + place, n), :]
            g = rmt[2, at(k), :] * (first + rmt[0, at(k), :] * alpha)
            if k == 0:
                alpha = last
            else:
                alpha = last + rmt[1, at(k), :] * (alpha + rmt[4, at(k - 1), :] * g)
            gs.append(g)
            alphas.append(alpha)
        after = jnp.zeros((n, LX), f32)
        dst[pl.ds(0, n), :] = after
        for k in range(NR - 1, -1, -1):
            dst[pl.ds(k * size + place, n), :] = after
            if k + 1 < NR:
                dst[pl.ds((k + 1) * size, n), :] = alphas[k] + rmt[4, at(k), :] * after
            after = gs[k] + rmt[3, at(k), :] * after

    receiveb1()
    close_radial(rb1, sb2, QB, F * G, F * G, lambda k: pl.ds(k * QA, F * G))
    sendb2()

    receive2()
    ys, y = [], None
    for i in range(CR):
        v = r2[pl.ds(i * QA, QA), :] * rline[0, i]
        y = v if y is None else v + rline[1, i] * y
        ys.append(y)
    eloc[CR - 1] = y
    for s in range(3):
        s3[pl.ds(4 + s, NR, stride=QE), :] = y[8 * s : 8 * s + 8]
    for i in range(CR - 2, -1, -1):
        y = ys[i] + rline[2, i] * y
        eloc[i] = y
    for s in range(3):
        s3[pl.ds(s, NR, stride=QE), :] = y[8 * s : 8 * s + 8]
    send3()
    receive3()
    close_radial(r3, s4, QE, 3, 4, lambda k: pl.ds(k * QA + ir, 3, stride=8))
    send4()

    receiveb2()
    for f in range(F):
        lefts = [rtab[3, f], rtab[4, f]]
        for a in range(CA):
            g, o = a // 8, a % 8
            sides = [
                jnp.broadcast_to(rb2[pl.ds(o * QB + v * F * G + g * F + f, 1), :], (CR, LX)) for v in range(2)
            ]
            x[f, a] = x[f, a] + lefts[0] * sides[0] + lefts[1] * sides[1]

    receive4()
    before = jnp.concatenate([r4[pl.ds(s, NR, stride=QE), :] for s in range(3)], axis=0)
    behind = jnp.concatenate([r4[pl.ds(4 + s, NR, stride=QE), :] for s in range(3)], axis=0)
    for i in range(CR):
        re[pl.ds(i * QA, QA), :] = eloc[i] + rline[3, i] * before + rline[4, i] * behind
    for f in range(F):
        enter = [re[pl.ds(v * F + f, CR, stride=QA), :] for v in range(NV)]
        for a in range(CA):
            total = x[f, a] + row(ktab, 0, f, a) * enter[0] + row(ktab, 1, f, a) * enter[1]
            out[f, a] = total + row(ktab, 2, f, a) * enter[2] + row(ktab, 3, f, a) * enter[3]

    for copy in edge_out:
        copy.wait_send()
    halo.wait_send()
    for finish in (finish1, finish2, finishb1, finishb2, finish3, finish4):
        finish()


def local(residual, left_vec, dissip, azim_coef, radial_coef):
    vm = pltpu.VMEM
    dma = pltpu.SemaphoreType.DMA
    hbm = pl.BlockSpec(memory_space=pltpu.HBM)
    return pl.pallas_call(
        body,
        out_shape=jax.ShapeDtypeStruct((F, CA, CR, LX), f32),
        in_specs=[hbm] * 5,
        out_specs=pl.BlockSpec(memory_space=pltpu.VMEM),
        scratch_shapes=[
            vm((F, CA, CR, LX), f32),
            pltpu.SMEM((F, F), f32), pltpu.SMEM((F,), f32),
            vm((F, 4, NA * CA), f32), vm((F, 2, NR * CR), f32),
            vm((4, 8, NA * CA), f32), vm((48, LX), f32),
            vm((2 * CR, LX), f32), vm((2 * CR, LX), f32),
            vm((NA, 1, LX), f32), vm((NA, 1, LX), f32),
            vm((4, NA * CA, 8), f32),
            vm((2, NR * CR, QA), f32), vm((2, QA, NR * CR), f32),
            vm((6, F, CA, LX), f32),
            vm((NV, CA * NA, 8), f32),
            vm((NV, F, CA, LX), f32),
            vm((20, NA, 8, LX), f32),
            vm((5, CR * NR, QA), f32),
            vm((5, F, CR, LX), f32),
            vm((5, CR, QA, LX), f32),
            vm((5, NR * QA, LX), f32),
            *[vm((NA * QA, LX), f32)] * 4,
            *[vm((NR * QB, LX), f32)] * 4,
            *[vm((NR * QE, LX), f32)] * 4,
            vm((CR, QA, LX), f32), vm((CR * QA, LX), f32),
            dma((5,)), dma((2,)),
            *[dma((NA,))] * 6,
            *[dma((NR,))] * 8,
        ],
        compiler_params=pltpu.CompilerParams(
            collective_id=0, has_side_effects=True, vmem_limit_bytes=63438848
        ),
        name="adi",
    )(
        residual, left_vec, dissip,
        jnp.transpose(azim_coef, (1, 0, 2)), jnp.transpose(radial_coef, (1, 0, 2)),
    )


def solution(mesh):
    placed = (P(None, "azim", "rad", "axial"), P(), P(), P(), P())
    return jax.shard_map(
        local,
        mesh=mesh,
        in_specs=placed,
        out_specs=P(None, "azim", "rad", "axial"),
        check_vma=False,
    )
```

time: 48.9 us -> 40.6 us (0.83)
  Pallas kernels: 43.4 us -> 37.9 us
  local copies, waits for them, and re-layouts: 5.2 us -> 2.51 us
    pallas_call x1, Pallas kernels: 43.4 us -> 37.9 us  [local(): pl.pallas_call(body, out_shape=jax.ShapeDtypeStruct((F, CA, CR, LX), f32)...]
    unnamed x9 -> x1, local copies, waits for them, and re-layouts: 5.2 us -> 2.51 us
where the time goes in v2:
time: 40.6 us; the launch traced here: 40.5 us
  Pallas kernels  37.9 us (93%)
  local copies, waits for them, and re-layouts  2.51 us (6%)
    pallas_call x1, Pallas kernels, local(): pl.pallas_call(body, out_shape=jax.ShapeDtypeStruct((F, CA, CR, LX), f32)...  37.9 us
    unnamed x1, local copies, waits for them, and re-layouts  2.51 us

profile of v2, /device:TPU:1, one launch (start us, length us, event | category | flops | bytes accessed | tf_op | source)
XLA Modules:
  0.0 40.5 jit_solution(16835059119171697348)
XLA Ops:
  0.0 37.9 %adi.1 = f32[5,32,16,128]{3,2,1,0:T(8,128)} custom-call(f32[5,32,16,128]{3,2,1,0:T(8,128)} %res_hbm.1, f32[5,5]{1,0:T(8,128)} %lv_hbm.1, f32[5]{0:T(128)} %dis_hbm.1, f32[5,4,512]{2,1,0:T(4,128)} %bitcast.2, f32[5,2,128]{2,1,0:T(2,128)} %bitcast.3), custom_call_target="tpu_custom_call" | custom-call | tf_op jit(solution)/shard_map/adi/pallas_call | solution.py:478
  37.9 2.5 %copy.7 = f32[5,32,16,128]{3,2,1,0:T(8,128)} copy(f32[5,32,16,128]{3,2,1,0:T(8,128)} %adi.1) | data formatting | bytes 2621440
